TPU v7x, 512 devices: a whole 4x4x16 slice. The times are simulated.
512 devices in a mesh: neuron: 128 (over z, y, core), trial: 4 (over x).
Axes of the slice: x: 4, y: 4, z: 16, core: 2. Of those that a mesh axis runs over, the one named last changes fastest.
Arguments:
- tensor: bfloat16 [8, 16384, 1024], P('trial', 'neuron'), may hold values from -1000 to 1000
- time_init: float32 [32, 1024], replicated, may hold values from -6 to 6
- trial_init: float32 [32, 8], P(None, 'trial'), may hold values from -6 to 6
Outputs:
- neuron_factor: float32 [32, 16384], P(None, 'neuron')
- time_factor: float32 [32, 1024], P(None, ('neuron', 'trial'))
- trial_factor: float32 [32, 8], P(None, 'trial')
All inputs are finite; a program needn't handle non-finite values.
Results may differ from a plain program's by a relative error of at most 0.011.
Values may be sent and summed in bfloat16 or wider, within the bound.
No kernel may reach another device: no remote copies, remote signals or barrier semaphores. Data moves between devices by JAX's collectives and lax.ppermute only.
A program may use at most 64 MiB of HBM per device.

v0:
```python
import jax
import jax.numpy as jnp
from jax import lax
from jax.sharding import PartitionSpec as P

SWEEPS = 2
ridge_share = 0.1
tiny_eps = 1e-06


def gram_of(matrix):
    return lax.dot_general(
        matrix,
        matrix,
        (((1,), (1,)), ((), ())),
        precision=lax.Precision.HIGHEST,
        preferred_element_type=jnp.float32,
    )


def damped_solve(gram_mat, right_hand):
    order_size = gram_mat.shape[0]
    identity_mat = jnp.eye(order_size, dtype=jnp.float32)
    damped = gram_mat + ridge_share * (jnp.trace(gram_mat) / order_size) * identity_mat
    cholesky_low = jnp.linalg.cholesky(damped)
    return jax.scipy.linalg.cho_solve((cholesky_low, True), right_hand)


def per_device(tensor, time_init, trial_init):
    timepoints = tensor.shape[2]
    component_count = time_init.shape[0]
    neuron_count = tensor.shape[1] * lax.axis_size("neuron")
    devices = lax.axis_size("neuron") * lax.axis_size("trial")
    share_width = timepoints // devices
    position = lax.axis_index(("neuron", "trial"))

    def trial_gram_of(trial_cols):
        return gram_of(lax.all_gather(trial_cols, "trial", axis=1, tiled=True))

    trial_now = trial_init
    trial_gram = trial_gram_of(trial_now)
    time_gram = gram_of(time_init)
    time_rounded = time_init.astype(jnp.bfloat16)
    time_out = lax.dynamic_slice_in_dim(time_init, position * share_width, share_width, 1)
    neuron_now = jnp.zeros((component_count, tensor.shape[1]), jnp.float32)
    for sweep_index in range(SWEEPS):
        projected = jnp.einsum(
            "rj,kij->kri", time_rounded, tensor, preferred_element_type=jnp.float32
        )
        local_terms = jnp.sum(trial_now.T[:, :, None] * projected, axis=0)
        neuron_terms = lax.psum(local_terms, "trial")
        neuron_raw = damped_solve(trial_gram * time_gram, neuron_terms)
        squares = lax.psum(jnp.sum(neuron_raw * neuron_raw, axis=1), "neuron")
        scaling = 1.0 / jnp.sqrt(squares / neuron_count + tiny_eps)
        neuron_now = neuron_raw * scaling[:, None]
        neuron_gram, trial_terms = lax.psum(
            (gram_of(neuron_now), jnp.sum(neuron_now[None] * projected, axis=2).T), "neuron"
        )
        trial_now = damped_solve(neuron_gram * time_gram, trial_terms)
        trial_gram = trial_gram_of(trial_now)
        weights = (neuron_now[None] * trial_now.T[:, :, None]).astype(jnp.bfloat16)
        time_local = jnp.einsum("kri,kij->rj", weights, tensor, preferred_element_type=jnp.float32)
        time_system = neuron_gram * trial_gram
        time_terms = lax.psum(time_local, ("neuron", "trial"))
        time_raw = damped_solve(time_system, time_terms)
        time_now = time_raw / jnp.sqrt(
            jnp.mean(time_raw * time_raw, axis=1, keepdims=True) + tiny_eps
        )
        time_gram = gram_of(time_now)
        time_rounded = time_now.astype(jnp.bfloat16)
        time_out = lax.dynamic_slice_in_dim(time_now, position * share_width, share_width, 1)
    return (neuron_now, time_out, trial_now)


def solution(mesh):
    placed = (P("trial", "neuron", None), P(), P(None, "trial"))
    return jax.shard_map(
        per_device,
        mesh=mesh,
        in_specs=placed,
        out_specs=(P(None, "neuron"), P(None, ("neuron", "trial")), P(None, "trial")),
        check_vma=False,
    )
```

profile of v0, /device:TPU:1, one launch (start us, length us, event | category | flops | bytes accessed | tf_op | source)
XLA Modules:
  0.0 2487.0 jit_solution(9856906988820335533)
XLA Ops:
  7.2 1.3 fusion.51
  8.5 8.7 all-gather
  17.2 0.8 select_reduce_fusion.8
  18.8 2.9 cholesky.104
  21.7 0.6 compare_reduce_fusion.5
  22.4 0.7 fusion.5
  23.0 2.4 custom-call.20
  25.8 11.0 psum.70
  37.3 259.1 %psum.71 = f32[32]{0:T(128)S(1)} all-reduce(f32[32]{0:T(128)S(1)} %get-tuple-element.29), channel_id=1, replica_groups=mesh['neuron'=128,'trial'=4] {'neuron'}, use_global_device_ids=true, to_apply=%region_6.9 | all-reduce | flops 32 | bytes 256 | tf_op jit(solution)/shard_map/psum | solution.py:53
  296.7 485.7 %all-reduce.1 = (f32[32,2]{0,1:T(2,128)S(1)}, f32[32,32]{0,1:T(8,128)S(1)}) all-reduce(f32[32,2]{0,1:T(2,128)S(1)} %bitcast.141, f32[32,32]{0,1:T(8,128)S(1)} %fusion.52), channel_id=1, replica_groups=mesh['neuron'=128,'trial'=4] {'neuron'}, use_global_device_ids=true, to_apply=%region_10.13 | all-reduce | flops 1088 | bytes 8704 | tf_op jit(solution)/shard_map/psum | solution.py:56
  782.4 0.6 select_reduce_fusion.7
  783.8 2.9 cholesky.115
  786.7 0.6 compare_reduce_fusion.4
  787.3 0.7 fusion.6
  788.0 2.4 custom-call.21
  790.9 0.9 convolution_bitcast_fusion.1
  791.9 6.2 all-gather.1
  798.1 0.8 select_reduce_fusion.6
  799.7 2.9 cholesky.126
  802.6 0.6 compare_reduce_fusion.3
  803.3 0.7 fusion.7
  803.9 2.4 custom-call.22
  806.4 440.6 %all-reduce.5.cloned.1.call-done = f32[32,1024]{1,0:T(8,128)} async-done(((f32[32,1024]{1,0:T(8,128)}), f32[32,1024]{1,0:T(8,128)}) %all-reduce.5.cloned.1.call-update) | async-done | bytes 131088 | tf_op jit(solution)/shard_map/psum | solution.py:64
  1246.9 1.2 fusion.28
  1248.8 1.0 select_reduce_fusion.5
  1250.5 2.9 cholesky.137
  1253.5 0.6 compare_reduce_fusion.2
  1254.1 0.7 fusion.8
  1254.8 2.4 custom-call.23
  1257.2 12.2 psum.75
  1269.8 249.2 %psum.76 = f32[32]{0:T(128)S(1)} all-reduce(f32[32]{0:T(128)S(1)} %get-tuple-element.37), channel_id=1, replica_groups=mesh['neuron'=128,'trial'=4] {'neuron'}, use_global_device_ids=true, to_apply=%region_18.23 | all-reduce | flops 32 | bytes 256 | tf_op jit(solution)/shard_map/psum | solution.py:53
  1519.3 485.9 %all-reduce = (f32[32,2]{0,1:T(2,128)S(1)}, f32[32,32]{0,1:T(8,128)S(1)}) all-reduce(f32[32,2]{0,1:T(2,128)S(1)} %bitcast.142, f32[32,32]{0,1:T(8,128)S(1)} %fusion.53), channel_id=1, replica_groups=mesh['neuron'=128,'trial'=4] {'neuron'}, use_global_device_ids=true, to_apply=%region_22.27 | all-reduce | flops 1088 | bytes 8704 | tf_op jit(solution)/shard_map/psum | solution.py:56
  2005.2 0.6 select_reduce_fusion.4
  2006.6 2.9 cholesky.148
  2009.5 0.6 compare_reduce_fusion.1
  2010.2 0.7 fusion.9
  2010.8 2.4 custom-call.24
  2013.7 5.3 all-gather.2
  2019.0 0.8 select_reduce_fusion.3
  2020.5 2.9 cholesky.159
  2023.5 0.6 compare_reduce_fusion
  2024.1 0.9 convolution_bitcast_fusion
  2025.0 0.7 fusion.10
  2025.7 2.4 custom-call.25
  2028.1 449.7 %all-reduce.7.cloned.1.call-done = f32[32,1024]{1,0:T(8,128)} async-done(((f32[32,1024]{1,0:T(8,128)}), f32[32,1024]{1,0:T(8,128)}) %all-reduce.7.cloned.1.call-update) | async-done | bytes 131088 | tf_op jit(solution)/shard_map/psum | solution.py:64
  2477.9 1.2 fusion.13
  2479.1 0.4 multiply_reduce_fusion
  2479.6 0.6 copy.39
  (60 shorter events, 4.3 us)
Async XLA Ops:
  7.2 18.3 copy-start
  7.2 1239.8 %all-reduce.5.cloned.1.call-start = ((), (), s32[]{:S(2)}) async-start(), calls=%async_computation | async-start | bytes 262144 | tf_op jit(solution)/shard_map/psum | solution.py:64
  7.2 1.3 copy-start.4
  8.5 16.9 copy-start.1
  791.8 1686.1 %all-reduce.7.cloned.1.call-start = ((), (), s32[]{:S(2)}) async-start(), calls=%async_computation.1 | async-start | bytes 262144 | tf_op jit(solution)/shard_map/psum | solution.py:64
  1519.1 505.0 %copy-start.2 = (f32[32,128]{1,0:T(8,128)}, f32[32,128]{1,0:T(8,128)S(1)}, u32[]{:S(2)}) copy-start(f32[32,128]{1,0:T(8,128)S(1)} %broadcast_multiply_fusion) | copy-start | bytes 49156
  2013.7 10.4 copy-start.3
Sparse Core Ops, SparseCore 0:
  791.9 454.9 all-reduce.4
  2025.2 452.6 all-reduce.6
where the time goes:
time: 2490 us
  blocking collectives  1520 us (61%)
  waiting for transfers between devices  890 us (36%)
  other arithmetic  41.8 us (2%)
    psum x2, blocking collectives, per_device(): lax.psum((gram_of(neuron_now), jnp.sum(neuron_now[None] * projected, axis...  972 us
    psum x2, waiting for transfers between devices, per_device(): time_terms = lax.psum(time_local, ('neuron', 'trial'))  890 us
    psum x2, blocking collectives, per_device(): squares = lax.psum(jnp.sum(neuron_raw * neuron_raw, axis=1), 'neuron')  508 us
  transfers between devices with their start and end apart: 2, of which 2 were waited for; matrix products, arithmetic and copies ran while one was open for 0% of the time, Pallas kernels for 0%

commit v1 on v0

--- a/solution.py
+++ b/solution.py
@@ -61,7 +61,7 @@
         weights = (neuron_now[None] * trial_now.T[:, :, None]).astype(jnp.bfloat16)
         time_local = jnp.einsum("kri,kij->rj", weights, tensor, preferred_element_type=jnp.float32)
         time_system = neuron_gram * trial_gram
-        time_terms = lax.psum(time_local, ("neuron", "trial"))
+        time_terms = lax.psum(lax.psum(time_local, "trial"), "neuron")
         time_raw = damped_solve(time_system, time_terms)
         time_now = time_raw / jnp.sqrt(
             jnp.mean(time_raw * time_raw, axis=1, keepdims=True) + tiny_eps

time: 2490 us -> 2350 us (0.944)
  waiting for transfers between devices: 890 us -> 746 us
    psum x2 -> x4, waiting for transfers between devices: 890 us -> 746 us  [per_device(): time_terms = lax.psum(lax.psum(time_local, 'trial'), 'neuron')]
  transfers between devices with their start and end apart: 2 -> 4, of which waited for: 2 -> 4; matrix products, arithmetic and copies ran while one was open for 0% -> 0% of each run, Pallas kernels for 0% -> 0%
where the time goes in v1:
time: 2350 us
  blocking collectives  1530 us (65%)
  waiting for transfers between devices  746 us (32%)
  other arithmetic  41.8 us (2%)
    psum x2, blocking collectives, per_device(): lax.psum((gram_of(neuron_now), jnp.sum(neuron_now[None] * projected, axis...  972 us
    psum x4, waiting for transfers between devices, per_device(): time_terms = lax.psum(lax.psum(time_local, 'trial'), 'neuron')  746 us
    psum x2, blocking collectives, per_device(): squares = lax.psum(jnp.sum(neuron_raw * neuron_raw, axis=1), 'neuron')  511 us
  transfers between devices with their start and end apart: 4, of which 4 were waited for; matrix products, arithmetic and copies ran while one was open for 0% of the time, Pallas kernels for 0%

profile of v1, /device:TPU:1, one launch (start us, length us, event | category | flops | bytes accessed | tf_op | source)
XLA Modules:
  0.0 2346.4 jit_solution(16221688963698033494)
XLA Ops:
  7.2 1.3 fusion.51
  8.5 8.7 all-gather
  17.2 0.8 select_reduce_fusion.8
  18.8 2.9 cholesky.104
  21.7 0.6 compare_reduce_fusion.5
  22.4 0.7 fusion.5
  23.0 2.4 custom-call.20
  25.8 11.0 psum.84
  37.3 259.1 %psum.85 = f32[32]{0:T(128)S(1)} all-reduce(f32[32]{0:T(128)S(1)} %get-tuple-element.29), channel_id=1, replica_groups=mesh['neuron'=128,'trial'=4] {'neuron'}, use_global_device_ids=true, to_apply=%region_6.9 | all-reduce | flops 32 | bytes 256 | tf_op jit(solution)/shard_map/psum | solution.py:53
  296.7 485.7 %all-reduce.1 = (f32[32,2]{0,1:T(2,128)S(1)}, f32[32,32]{0,1:T(8,128)S(1)}) all-reduce(f32[32,2]{0,1:T(2,128)S(1)} %bitcast.141, f32[32,32]{0,1:T(8,128)S(1)} %fusion.52), channel_id=1, replica_groups=mesh['neuron'=128,'trial'=4] {'neuron'}, use_global_device_ids=true, to_apply=%region_10.13 | all-reduce | flops 1088 | bytes 8704 | tf_op jit(solution)/shard_map/psum | solution.py:56
  783.8 2.9 cholesky.115
  786.7 0.6 compare_reduce_fusion.4
  787.3 0.7 fusion.6
  788.0 2.4 custom-call.21
  790.9 0.9 convolution_bitcast_fusion.1
  791.9 6.2 all-gather.1
  798.1 0.8 select_reduce_fusion.6
  799.7 2.9 cholesky.126
  802.6 0.6 compare_reduce_fusion.3
  803.3 41.8 %all-reduce.7.cloned.1.call-done = f32[32,1024]{1,0:T(8,128)} async-done(((f32[32,1024]{1,0:T(8,128)}), f32[32,1024]{1,0:T(8,128)}) %all-reduce.7.cloned.1.call-update) | async-done | bytes 131088 | tf_op jit(solution)/shard_map/psum | solution.py:64
  845.1 0.7 fusion.7
  845.8 2.4 custom-call.22
  848.2 326.9 %all-reduce.9.cloned.1.call-done = f32[32,1024]{1,0:T(8,128)} async-done(((f32[32,1024]{1,0:T(8,128)}), f32[32,1024]{1,0:T(8,128)}) %all-reduce.9.cloned.1.call-update) | async-done | bytes 131088 | tf_op jit(solution)/shard_map/psum | solution.py:64
  1175.1 1.2 fusion.28
  1176.9 1.0 select_reduce_fusion.5
  1178.6 2.9 cholesky.137
  1181.6 0.6 compare_reduce_fusion.2
  1182.2 0.7 fusion.8
  1182.9 2.4 custom-call.23
  1185.3 13.3 psum.90
  1199.1 252.3 %psum.91 = f32[32]{0:T(128)S(1)} all-reduce(f32[32]{0:T(128)S(1)} %get-tuple-element.37), channel_id=1, replica_groups=mesh['neuron'=128,'trial'=4] {'neuron'}, use_global_device_ids=true, to_apply=%region_19.24 | all-reduce | flops 32 | bytes 256 | tf_op jit(solution)/shard_map/psum | solution.py:53
  1451.7 485.9 %all-reduce = (f32[32,2]{0,1:T(2,128)S(1)}, f32[32,32]{0,1:T(8,128)S(1)}) all-reduce(f32[32,2]{0,1:T(2,128)S(1)} %bitcast.142, f32[32,32]{0,1:T(8,128)S(1)} %fusion.53), channel_id=1, replica_groups=mesh['neuron'=128,'trial'=4] {'neuron'}, use_global_device_ids=true, to_apply=%region_23.28 | all-reduce | flops 1088 | bytes 8704 | tf_op jit(solution)/shard_map/psum | solution.py:56
  1937.6 0.6 select_reduce_fusion.4
  1939.0 2.9 cholesky.148
  1941.9 0.6 compare_reduce_fusion.1
  1942.6 0.7 fusion.9
  1943.2 2.4 custom-call.24
  1946.1 5.3 all-gather.2
  1951.4 0.8 select_reduce_fusion.3
  1952.9 2.9 cholesky.159
  1955.9 0.9 convolution_bitcast_fusion
  1956.9 0.6 compare_reduce_fusion
  1957.5 50.2 %all-reduce.11.cloned.1.call-done = f32[32,1024]{1,0:T(8,128)} async-done(((f32[32,1024]{1,0:T(8,128)}), f32[32,1024]{1,0:T(8,128)}) %all-reduce.11.cloned.1.call-update) | async-done | bytes 131088 | tf_op jit(solution)/shard_map/psum | solution.py:64
  2007.8 0.7 fusion.10
  2008.4 2.4 custom-call.25
  2010.9 326.7 %all-reduce.13.cloned.1.call-done = f32[32,1024]{1,0:T(8,128)} async-done(((f32[32,1024]{1,0:T(8,128)}), f32[32,1024]{1,0:T(8,128)}) %all-reduce.13.cloned.1.call-update) | async-done | bytes 131088 | tf_op jit(solution)/shard_map/psum | solution.py:64
  2337.5 1.2 fusion.13
  2339.2 0.6 copy.39
  (66 shorter events, 5.4 us)
Async XLA Ops:
  7.2 18.3 copy-start
  7.2 837.9 %all-reduce.7.cloned.1.call-start = ((), (), s32[]{:S(2)}) async-start(), calls=%async_computation | async-start | bytes 262144 | tf_op jit(solution)/shard_map/psum | solution.py:64
  7.2 1.3 copy-start.4
  8.5 16.9 copy-start.1
  791.8 383.3 %all-reduce.9.cloned.1.call-start = ((), (), s32[]{:S(2)}) async-start(), calls=%async_computation.1 | async-start | bytes 262144 | tf_op jit(solution)/shard_map/psum | solution.py:64
  845.1 1162.7 %all-reduce.11.cloned.1.call-start = ((), (), s32[]{:S(2)}) async-start(), calls=%async_computation.2 | async-start | bytes 262144 | tf_op jit(solution)/shard_map/psum | solution.py:64
  1451.5 504.4 %copy-start.2 = (f32[32,128]{1,0:T(8,128)}, f32[32,128]{1,0:T(8,128)S(1)}, u32[]{:S(2)}) copy-start(f32[32,128]{1,0:T(8,128)S(1)} %broadcast_multiply_fusion) | copy-start | bytes 49156
  1946.1 9.8 copy-start.3
  1956.8 380.8 %all-reduce.13.cloned.1.call-start = ((), (), s32[]{:S(2)}) async-start(), calls=%async_computation.3 | async-start | bytes 262144 | tf_op jit(solution)/shard_map/psum | solution.py:64
Sparse Core Ops, SparseCore 0:
  791.9 53.0 all-reduce.6
  848.5 326.5 all-reduce.8
  1956.9 50.7 all-reduce.10
  2011.0 326.4 all-reduce.12
